TPU v7x, 256 devices: a whole 4x4x8 slice. The times are simulated.
256 devices in a mesh: seq: 32 (over z, y), mp: 4 (over x), req: 2 (over core).
Axes of the slice: x: 4, y: 4, z: 8, core: 2. Of those that a mesh axis runs over, the one named last changes fastest.
Arguments:
- hidden: bfloat16 [2, 8192, 3072], P('req', 'seq', 'mp'), may hold values from -6 to 6
- norm_gain: bfloat16 [3072], replicated, may hold values from 0.5 to 1.5
- w_query: bfloat16 [3072, 1024], P(None, 'mp'), may hold values from -0.109375 to 0.109375
- w_keyval: bfloat16 [3072, 512], P(None, 'mp'), may hold values from -0.109375 to 0.109375
- w_attn_out: bfloat16 [1024, 3072], P('mp'), may hold values from -1.5 to 1.5
- w_inner: bfloat16 [3072, 2, 1536], P(None, None, 'mp'), may hold values from -0.109375 to 0.109375
- w_bc: bfloat16 [3072, 512], P(None, 'mp'), may hold values from -0.109375 to 0.109375
- w_dt: bfloat16 [3072, 12], P(None, 'mp'), may hold values from -0.109375 to 0.109375
- dt_bias: float32 [12], P('mp'), may hold values from -4 to 0
- a_log: float32 [12], P('mp'), may hold values from -12 to 0
- d_skip: float32 [12], P('mp'), may hold values from 0.1 to 10
- conv_x: bfloat16 [4, 1536], P(None, 'mp'), may hold values from -3 to 3
- conv_bc: bfloat16 [4, 512], replicated, may hold values from -3 to 3
- mamba_gain: bfloat16 [1536], P('mp'), may hold values from 0.5 to 1.5
- w_mamba_out: bfloat16 [1536, 3072], P('mp'), may hold values from -0.15625 to 0.15625
- cache: bfloat16 [2, 8192, 512], P('req', 'seq', 'mp'), may hold values from -70 to 70, as said below
- cache_len: int32 [2], P('req'), may hold values from 256 to 8192
- tail_x: bfloat16 [2, 3, 1536], P('req', None, 'mp'), may hold values from -6 to 6
- tail_bc: bfloat16 [2, 3, 512], P('req'), may hold values from -6 to 6
- ssm_init: float32 [2, 12, 128, 256], P('req', 'mp'), may hold values from -6 to 6
Outputs:
- layer_out: bfloat16 [2, 8192, 3072], P('req', 'seq', 'mp')
- new_keyval: bfloat16 [2, 8192, 512], P('req', 'seq', 'mp')
- block_states: float32 [2, 32, 12, 128, 256], P('req', 'seq', 'mp')
Inputs may be any that keep to these rules, and one draw needn't show every extreme that they name: Rows of the cache at or past cache_len are unused.
All inputs are finite; a program needn't handle non-finite values.
Results may differ from a plain program's by a relative error of at most 0.0097.
Values may be sent and summed in bfloat16 or wider, within the bound.
A program may use at most 192 MiB of HBM per device.

v0:
```python
import jax
import jax.numpy as jnp
from jax import lax
from jax.sharding import PartitionSpec as P

HD = 128
QH = 8
KVH = 2
NS = 256
CONV = 4
epsilon = 1e-05
rope_base = 100000000000.0
negative = -1e30


def shifted(block, axis, distance):
    devices = range(lax.axis_size(axis))
    route = [(i - distance, i) for i in devices if i - distance in devices]
    return lax.ppermute(block, axis, route)


def prefix(part, axis, combine, identity):
    place = lax.axis_index(axis)
    gathered = jax.tree.map(lambda a: lax.all_gather(a, axis), part)
    state = jax.tree.map(lambda a, e: jnp.zeros_like(a) + jnp.asarray(e, a.dtype), part, identity)

    def one(turn, state):
        return combine(
            state, jax.tree.map(lambda a: lax.dynamic_index_in_dim(a, turn, 0, False), gathered)
        )

    return lax.fori_loop(0, place, one, state)


def rotate(values, positions):
    half = HD // 2
    freqs = rope_base ** (-jnp.arange(half, dtype=jnp.float32) * 2.0 / HD)
    angles = positions.astype(jnp.float32)[:, None] * freqs[None, :]
    cosine = jnp.cos(angles)[:, None, :]
    sine = jnp.sin(angles)[:, None, :]
    first = values[..., :half]
    second = values[..., half:]
    return jnp.concatenate(
        [first * cosine - second * sine, second * cosine + first * sine], axis=-1
    )


def rms_scale(values):
    mean_sq = jnp.mean(values * values, axis=-1, keepdims=True)
    return values * lax.rsqrt(mean_sq + epsilon)


def causal_conv(tail, inputs, taps):
    padded = jnp.concatenate([tail, inputs], axis=0).astype(jnp.float32)
    count = inputs.shape[0]
    total = jnp.zeros(inputs.shape, jnp.float32)
    for offset in range(CONV):
        total = total + taps[offset].astype(jnp.float32)[None, :] * padded[offset : offset + count]
    return jax.nn.silu(total)


def join_states(earlier, later):
    return (earlier[0] * later[0], later[0][:, None, None] * earlier[1] + later[1])


def shards(
    hidden,
    norm_gain,
    w_query,
    w_keyval,
    w_attn_out,
    w_inner,
    w_bc,
    w_dt,
    dt_bias,
    a_log,
    d_skip,
    conv_x,
    conv_bc,
    mamba_gain,
    w_mamba_out,
    cache,
    cache_len,
    tail_x,
    tail_bc,
    ssm_init,
):
    high = lax.Precision.HIGHEST
    own_rows = hidden[0]
    tokens = own_rows.shape[0]
    seq_pos = lax.axis_index("seq")
    mp_pos = lax.axis_index("mp")
    length = cache_len[0]
    whole = lax.all_gather(own_rows, "mp", axis=1, tiled=True)
    normed = (rms_scale(whole.astype(jnp.float32)) * norm_gain.astype(jnp.float32)).astype(
        jnp.bfloat16
    )
    positions = length + seq_pos * tokens + jnp.arange(tokens, dtype=jnp.int32)
    local_heads = w_query.shape[1] // HD
    query = rotate(
        jnp.dot(normed, w_query, preferred_element_type=jnp.float32).reshape(
            tokens, local_heads, HD
        ),
        positions,
    ).astype(jnp.bfloat16)
    projected = jnp.dot(normed, w_keyval, preferred_element_type=jnp.float32)
    roped = rotate(projected[:, None, :], positions)[:, 0, :]
    kv_block = jnp.where(mp_pos % 2 == 0, roped, projected).astype(jnp.bfloat16)
    bc_block = jnp.dot(normed, w_bc, preferred_element_type=jnp.float32).astype(jnp.bfloat16)
    kv_all, bc_all, cache_all = (
        lax.all_gather(kv_block, "mp", axis=1, tiled=True),
        lax.all_gather(bc_block, "mp", axis=1, tiled=True),
        lax.all_gather(cache[0], "mp", axis=1, tiled=True),
    )
    inner = jnp.einsum("td,dkc->tkc", normed, w_inner, preferred_element_type=jnp.float32).astype(
        jnp.bfloat16
    )
    rim = CONV - 1
    prev_x, prev_bc = shifted((inner[tokens - rim :, 1], bc_all[tokens - rim :]), "seq", 1)
    first_block = seq_pos == 0
    prev_x = jnp.where(first_block, tail_x[0], prev_x)
    prev_bc = jnp.where(first_block, tail_bc[0], prev_bc)
    mamba_heads = dt_bias.shape[0]
    x_conv = causal_conv(prev_x, inner[:, 1], conv_x).reshape(tokens, mamba_heads, HD)
    bc_conv = causal_conv(prev_bc, bc_all, conv_bc)
    b_mat = bc_conv[:, :NS]
    c_mat = bc_conv[:, NS:]
    step_size = jax.nn.softplus(jnp.dot(normed, w_dt, preferred_element_type=jnp.float32) + dt_bias)
    log_decay = -step_size * jnp.exp(a_log)[None, :]
    cumulative = jnp.cumsum(log_decay, axis=0)
    pairs = jnp.dot(c_mat, b_mat.T, precision=high)
    gap = cumulative[:, None, :] - cumulative[None, :, :]
    token_ids = jnp.arange(tokens)
    lower = (token_ids[:, None] >= token_ids[None, :])[:, :, None]
    decay = jnp.where(lower, jnp.exp(jnp.where(lower, gap, 0.0)), 0.0)
    mixing = decay * pairs[:, :, None] * step_size[None, :, :]
    inner_out = jnp.einsum("tsh,shp->thp", mixing, x_conv, precision=high)
    to_end = jnp.exp(cumulative[-1][None, :] - cumulative) * step_size
    own_state = jnp.einsum("sh,shp,sn->hpn", to_end, x_conv, b_mat, precision=high)
    block_decay = jnp.exp(cumulative[-1])
    prior_decay, prior_state = prefix(
        (block_decay, own_state),
        "seq",
        join_states,
        (jnp.ones_like(block_decay), jnp.zeros_like(own_state)),
    )
    incoming = prior_state + prior_decay[:, None, None] * ssm_init[0]
    carried = jnp.exp(cumulative)[:, :, None] * jnp.einsum(
        "tn,hpn->thp", c_mat, incoming, precision=high
    )
    mamba_y = inner_out + carried + d_skip[None, :, None] * x_conv
    state_after = block_decay[:, None, None] * incoming + own_state
    gated = mamba_y * jax.nn.silu(inner[:, 0].astype(jnp.float32).reshape(tokens, mamba_heads, HD))
    mixed = (
        rms_scale(gated).reshape(tokens, mamba_heads * HD) * mamba_gain.astype(jnp.float32)
    ).astype(jnp.bfloat16)
    cache_rows = cache_all.shape[0]
    shard_rows = cache_rows + tokens
    local_rows = jnp.concatenate([cache_all, kv_all], axis=0)
    group = mp_pos * local_heads // (QH // KVH)
    query_index = seq_pos * tokens + jnp.arange(tokens, dtype=jnp.int32)
    scale = 1.0 / float(HD) ** 0.5
    piece = lax.all_gather(local_rows, "seq", axis=0, tiled=True)
    top = jnp.full((local_heads, tokens), negative, jnp.float32)
    piece = lax.dynamic_slice_in_dim(piece, group * 2 * HD, 2 * HD, 1)
    count = piece.shape[0]
    index = jnp.arange(count, dtype=jnp.int32)
    owner = index // shard_rows
    offset = index % shard_rows
    in_cache = offset < cache_rows
    slot_ok = in_cache & (owner * cache_rows + offset < length)
    new_index = owner * tokens + offset - cache_rows
    valid = slot_ok[None, :] | (~in_cache)[None, :] & (new_index[None, :] <= query_index[:, None])
    scores = (
        jnp.einsum("qhd,kd->hqk", query, piece[:, :HD], preferred_element_type=jnp.float32) * scale
    )
    masked = jnp.where(valid[None], scores, negative)
    new_top = jnp.maximum(top, jnp.max(masked, axis=-1))
    weights = jnp.where(valid[None], jnp.exp(masked - new_top[:, :, None]), 0.0)
    total = jnp.sum(weights, axis=-1)
    accum = jnp.einsum(
        "hqk,kd->hqd",
        weights.astype(jnp.bfloat16),
        piece[:, HD : 2 * HD],
        preferred_element_type=jnp.float32,
    )
    top, total, accum = (new_top, total, accum)
    attended = jnp.transpose(accum / total[:, :, None], (1, 0, 2)).reshape(tokens, local_heads * HD)
    attended = attended.astype(jnp.bfloat16)
    term = jnp.dot(attended, w_attn_out, preferred_element_type=jnp.float32)
    term = term + jnp.dot(mixed, w_mamba_out, preferred_element_type=jnp.float32)
    summed = lax.psum_scatter(term, "mp", scatter_dimension=1, tiled=True)
    layer = (summed + own_rows.astype(jnp.float32)).astype(jnp.bfloat16)
    return (layer[None], kv_block[None], state_after[None, None])


def solution(mesh):
    placed = (
        P("req", "seq", "mp"),
        P(),
        P(None, "mp"),
        P(None, "mp"),
        P("mp", None),
        P(None, None, "mp"),
        P(None, "mp"),
        P(None, "mp"),
        P("mp"),
        P("mp"),
        P("mp"),
        P(None, "mp"),
        P(),
        P("mp"),
        P("mp", None),
        P("req", "seq", "mp"),
        P("req"),
        P("req", None, "mp"),
        P("req", None, None),
        P("req", "mp", None, None),
    )
    return jax.shard_map(
        shards,
        mesh=mesh,
        in_specs=placed,
        out_specs=(P("req", "seq", "mp"), P("req", "seq", "mp"), P("req", "seq", "mp", None, None)),
        check_vma=False,
    )
```

profile of v0, /device:TPU:1, one launch (start us, length us, event | category | flops | bytes accessed | tf_op | source)
XLA Modules:
  0.0 449.3 jit_solution(8750988892536039679)
XLA Ops:
  11.0 31.7 %all-gather.10.cloned.1.call-done = bf16[1,256,3072]{2,1,0:T(8,128)(2,1)} async-done(((bf16[1,256,768]{2,1,0:T(8,128)(2,1)}), bf16[1,256,3072]{2,1,0:T(8,128)(2,1)}) %all-gather.10.cloned.1.call-update) | async-done | bytes 1572880 | tf_op jit(solution)/shard_map/all_gather | solution.py:94
  42.7 1.9 fusion.9
  44.7 1.9 fusion.11
  46.6 1.4 fusion.13
  51.6 3.1 collective-permute-start
  54.7 2.0 convolution_convert_fusion
  56.7 9.4 %all_gather.29 = bf16[256,512]{1,0:T(8,128)(2,1)S(1)} all-gather(bf16[256,128]{1,0:T(8,128)(2,1)S(1)} %convolution_convert_fusion), channel_id=1, replica_groups=mesh['seq'=32,'mp'=4,'req'=2] {'mp'}, dimensions={1}, use_global_device_ids=true | all-gather | bytes 327680 | tf_op jit(solution)/shard_map/all_gather | solution.py:112
  66.1 3.2 collective-permute-start.1
  69.9 1.0 maximum_convert_fusion.1
  71.8 1.3 fusion.46
  73.9 9.4 %all-gather = bf16[1,256,512]{1,2,0:T(8,128)(2,1)S(1)} all-gather(bf16[1,256,128]{1,2,0:T(8,128)(2,1)S(1)} %copy.52), channel_id=2, replica_groups=mesh['seq'=32,'mp'=4,'req'=2] {'mp'}, dimensions={2}, use_global_device_ids=true | all-gather | bytes 327680 | tf_op jit(solution)/shard_map/all_gather | solution.py:113
  83.3 2.3 fusion.100
  85.9 9.8 %all_gather.27 = bf16[256,512]{0,1:T(8,128)(2,1)S(1)} all-gather(bf16[256,128]{0,1:T(8,128)(2,1)S(1)} %fusion.63), channel_id=1, replica_groups=mesh['seq'=32,'mp'=4,'req'=2] {'mp'}, dimensions={1}, use_global_device_ids=true | all-gather | bytes 327680 | tf_op jit(solution)/shard_map/all_gather | solution.py:111
  97.4 1.3 multiply_cosine_fusion
  98.6 15.5 %and_or_fusion = pred[256,16384]{0,1:T(8,128)(4,1)} fusion(s32[256]{0:T(256)S(1)} %iota_add_fusion, s32[16384]{0:T(1024)S(1)} %fusion.82, pred[16384]{0:T(1024)(128)(4,1)S(1)} %get-tuple-element.110, pred[16384]{0:T(1024)(128)(4,1)S(1)} %get-tuple-element.109), kind=kLoop, calls=%fused_computation.9 | loop fusion | flops 12582912 | bytes 4293632 | tf_op jit(solution)/shard_map/or | solution.py:173
  114.1 1.9 copy.63
  116.0 2.6 fusion.101
  119.0 37.4 %all-gather.3 = f32[32,1,3]{2,1,0:T(1,128)} all-gather(f32[1,1,3]{2,1,0:T(1,128)S(1)} %bitcast.181), channel_id=1, replica_groups=mesh['seq'=32,'mp'=4,'req'=2] {'seq'}, dimensions={0}, use_global_device_ids=true | all-gather | bytes 396 | tf_op jit(solution)/shard_map/all_gather | solution.py:24
  156.4 1.7 subtract_convert_fusion
  158.5 39.1 %all-gather.12.cloned.1.call-done = f32[96,128,256]{2,1,0:T(8,128)} async-done(((f32[3,128,256]{2,1,0:T(8,128)}), f32[96,128,256]{2,1,0:T(8,128)}) %all-gather.12.cloned.1.call-update) | async-done | bytes 12582928 | tf_op jit(solution)/shard_map/all_gather | solution.py:24
  197.7 1.5 convolution_multiply_fusion
  199.2 2.5 multiply_reduce_fusion
  201.9 143.7 %all-gather.8.cloned.1.call-done = bf16[16384,512]{0,1:T(8,128)(2,1)} async-done(((bf16[512,512]{0,1:T(8,128)(2,1)}), bf16[16384,512]{0,1:T(8,128)(2,1)}) %all-gather.8.cloned.1.call-update) | async-done | bytes 16777232 | tf_op jit(solution)/shard_map/all_gather | solution.py:163
  345.7 17.5 %fusion = (f32[2,256]{1,0:T(2,128)S(1)}, f32[16384,256,2]{1,0,2:T(8,128)}) fusion(pred[256,16384]{0,1:T(8,128)(4,1)} %and_or_fusion, bf16[256,2,64]{2,0,1:T(8,128)(2,1)S(1)} %copy-done.8, bf16[256,2,64]{2,0,1:T(8,128)(2,1)S(1)} %copy-done.7, bf16[16384,512]{0,1:T(8,128)(2,1)} %all-gather.8.cloned.1.call-done, s32[]{:T(128)S(6)} %select_n.107), kind=kOutput, calls=%fused_computation.4 | convolution fusion | flops 2172911104 | bytes 42076164 | tf_op jit(solution)/shard_map/qhd,kd->hqk/dot_general | solution.py:175
  363.2 15.6 %fusion.1 = f32[2,256]{1,0:T(2,128)S(1)} fusion(f32[16384,256,2]{1,0,2:T(8,128)} %get-tuple-element.104, f32[2,256]{1,0:T(2,128)S(1)} %broadcast_maximum_fusion, pred[256,16384]{0,1:T(8,128)(4,1)} %and_or_fusion), kind=kLoop, calls=%fused_computation.5 | loop fusion | flops 41942528 | bytes 37752832 | tf_op jit(solution)/shard_map/reduce_sum | solution.py:180
  378.8 17.1 %fusion.27 = bf16[256,2,128]{0,2,1:T(8,128)(2,1)S(1)} fusion(f32[16384,256,2]{1,0,2:T(8,128)} %get-tuple-element.104, f32[2,256]{1,0:T(2,128)S(1)} %broadcast_maximum_fusion, pred[256,16384]{0,1:T(8,128)(4,1)} %and_or_fusion, bf16[16384,512]{0,1:T(8,128)(2,1)} %all-gather.8.cloned.1.call-done, s32[]{:T(128)S(6)} %add.229, f32[256,2]{0,1:T(2,128)S(1)} %bitcast.180), kind=kOutput, calls=%fused_computation.32 | convolution fusion | flops 2189557760 | bytes 42078212 | tf_op jit(solution)/shard_map/hqk,kd->hqd/dot_general | solution.py:181
  395.9 2.0 fusion.102
  397.9 2.7 convolution_add_fusion
  400.7 1.6 copy.64
  402.3 1.9 add_bitcast_fusion
  404.2 36.7 %reduce-scatter.2.cloned.1.call-done = f32[256,768]{1,0:T(8,128)} async-done(((f32[256,3072]{1,0:T(8,128)}), f32[256,768]{1,0:T(8,128)}) %reduce-scatter.2.cloned.1.call-update) | async-done | bytes 786448 | tf_op jit(solution)/shard_map/reduce_scatter | solution.py:192
  440.9 1.9 fusion.40
  (97 shorter events, 11.8 us)
Async XLA Ops:
  7.2 390.7 %copy-start = (bf16[384,3072]{1,0:T(8,128)(2,1)S(1)}, bf16[384,3072]{1,0:T(8,128)(2,1)}, u32[]{:S(2)}) copy-start(bf16[384,3072]{1,0:T(8,128)(2,1)} %param.36) | copy-start | bytes 7077892
  7.2 35.5 %all-gather.10.cloned.1.call-start = ((), (), s32[]{:S(2)}) async-start(), calls=%async_computation.3 | async-start | bytes 1966080 | tf_op jit(solution)/shard_map/all_gather | solution.py:94
  7.9 189.7 %all-gather.12.cloned.1.call-start = ((), (), s32[]{:S(2)}) async-start(), calls=%async_computation.4 | async-start | bytes 12976128 | tf_op jit(solution)/shard_map/all_gather | solution.py:24
  42.7 3.9 copy-start.18
  46.6 2.4 copy-start.1
  46.6 2.4 copy-start.10
  46.6 2.4 copy-start.17
  46.6 8.1 %copy-start.5 = (bf16[3072,128]{1,0:T(8,128)(2,1)S(1)}, bf16[3072,128]{1,0:T(8,128)(2,1)}, u32[]{:S(2)}) copy-start(bf16[3072,128]{1,0:T(8,128)(2,1)} %param.28) | copy-start | bytes 2359300
  48.1 21.8 %copy-start.12 = (bf16[1,3,384]{2,1,0:T(4,128)(2,1)S(1)}, bf16[1,3,384]{2,1,0:T(4,128)(2,1)}, u32[]{:S(2)}) copy-start(bf16[1,3,384]{2,1,0:T(4,128)(2,1)} %param.39) | copy-start | bytes 6916
  48.1 23.2 %copy-start.11 = (bf16[1,3,512]{2,1,0:T(4,128)(2,1)S(1)}, bf16[1,3,512]{2,1,0:T(4,128)(2,1)}, u32[]{:S(2)}) copy-start(bf16[1,3,512]{2,1,0:T(4,128)(2,1)} %param.40) | copy-start | bytes 9220
  51.6 20.1 %copy-start.13 = (f32[3]{0:T(128)}, f32[3]{0:T(128)S(1)}, u32[]{:S(2)}) copy-start(f32[3]{0:T(128)S(1)} %get-tuple-element.66) | copy-start | bytes 40
  51.6 18.3 %collective-permute-start = (bf16[3,384]{1,0:T(4,128)(2,1)S(1)}, bf16[3,384]{1,0:T(4,128)(2,1)S(1)}, u32[]{:S(2)}, u32[]{:S(2)}) collective-permute-start(bf16[3,384]{1,0:T(4,128)(2,1)S(1)} %slice_bitcast_fusion.1), channel_id=1, source_target_pairs={{0,8},{8,16},{16,24},{24,32},{32,40},{40,48},{48,56},{56,64},{64,7... | collective-permute-start | bytes 6920 | tf_op jit(solution)/shard_map/ppermute | solution.py:19
  66.0 7.7 %copy-start.9 = (bf16[1,256,128]{2,1,0:T(8,128)(2,1)S(1)}, bf16[1,256,128]{2,1,0:T(8,128)(2,1)}, u32[]{:S(2)}) copy-start(bf16[1,256,128]{2,1,0:T(8,128)(2,1)} %param.37) | copy-start | bytes 196612
  66.1 5.2 %collective-permute-start.1 = (bf16[3,512]{1,0:T(4,128)(2,1)S(1)}, bf16[3,512]{1,0:T(4,128)(2,1)S(1)}, u32[]{:S(2)}, u32[]{:S(2)}) collective-permute-start(bf16[3,512]{1,0:T(4,128)(2,1)S(1)} %slice.136), channel_id=1, source_target_pairs={{0,8},{8,16},{16,24},{24,32},{32,40},{40,48},{48,56},{56,64},{64,7... | collective-permute-start | bytes 9224 | tf_op jit(solution)/shard_map/ppermute | solution.py:19
  71.3 24.4 %copy-start.4 = (f32[256,384]{0,1:T(8,128)}, f32[256,384]{0,1:T(8,128)S(1)}, u32[]{:S(2)}) copy-start(f32[256,384]{0,1:T(8,128)S(1)} %copy.58) | copy-start | bytes 1179652
  71.4 25.2 %copy-start.16 = (bf16[384]{0:T(512)(128)(2,1)S(1)}, bf16[384]{0:T(512)(128)(2,1)}, u32[]{:S(2)}) copy-start(bf16[384]{0:T(512)(128)(2,1)} %param.35) | copy-start | bytes 2308
  73.0 272.6 %all-gather.8.cloned.1.call-start = ((), (), s32[]{:S(2)}) async-start(), calls=%async_computation.1 | async-start | bytes 17301504 | tf_op jit(solution)/shard_map/all_gather | solution.py:163
  85.9 9.8 %copy-start.6 = (bf16[256,128]{0,1:T(8,128)(2,1)}, bf16[256,128]{0,1:T(8,128)(2,1)S(1)}, u32[]{:S(2)}) copy-start(bf16[256,128]{0,1:T(8,128)(2,1)S(1)} %fusion.63) | copy-start | bytes 196612
  96.5 344.3 %reduce-scatter.2.cloned.1.call-start = ((), (), s32[]{:S(2)}) async-start(), calls=%async_computation.2 | async-start | bytes 3932160 | tf_op jit(solution)/shard_map/reduce_scatter | solution.py:192
  98.6 20.3 %copy-start.15 = (f32[3]{0:T(128)S(1)}, f32[3]{0:T(128)}, u32[]{:S(2)}) copy-start(f32[3]{0:T(128)} %get-tuple-element.67) | copy-start | bytes 40
  199.2 146.5 %copy-start.7 = (bf16[256,2,64]{2,0,1:T(8,128)(2,1)S(1)}, bf16[256,2,64]{2,0,1:T(8,128)(2,1)}, u32[]{:S(2)}) copy-start(bf16[256,2,64]{2,0,1:T(8,128)(2,1)} %get-tuple-element.86) | copy-start | bytes 196612
  199.2 146.5 %copy-start.8 = (bf16[256,2,64]{2,0,1:T(8,128)(2,1)S(1)}, bf16[256,2,64]{2,0,1:T(8,128)(2,1)}, u32[]{:S(2)}) copy-start(bf16[256,2,64]{2,0,1:T(8,128)(2,1)} %get-tuple-element.87) | copy-start | bytes 196612
  397.9 2.7 copy-start.14
  397.9 4.4 copy-start.2
  400.6 40.2 %copy-start.3 = (bf16[1,256,768]{2,1,0:T(8,128)(2,1)S(1)}, bf16[1,256,768]{2,1,0:T(8,128)(2,1)}, u32[]{:S(2)}) copy-start(bf16[1,256,768]{2,1,0:T(8,128)(2,1)} %param.22) | copy-start | bytes 1179652
Sparse Core Ops, SparseCore 0:
  9.8 32.8 all-gather.9
  73.2 124.4 all-gather.11
  200.1 145.5 all-gather.7
  400.8 40.0 reduce-scatter.1
where the time goes:
time: 452 us; the launch traced here: 449 us
  waiting for transfers between devices  252 us (56%)
  blocking collectives  65.9 us (15%)
  matrix products  53.8 us (12%)
  other arithmetic  50.4 us (11%)
  between operations  14.9 us (3%)
  starting transfers between devices  6.45 us (1%)
  local copies, waits for them, and re-layouts  5.89 us (1%)
    all_gather x1, waiting for transfers between devices, shards(): piece = lax.all_gather(local_rows, 'seq', axis=0, tiled=True)  144 us
    all_gather x1, waiting for transfers between devices, prefix(): gathered = jax.tree.map(lambda a: lax.all_gather(a, axis), part)  39.1 us
    all_gather x1, blocking collectives, prefix(): gathered = jax.tree.map(lambda a: lax.all_gather(a, axis), part)  37.4 us
    reduce_scatter x1, waiting for transfers between devices, shards(): summed = lax.psum_scatter(term, 'mp', scatter_dimension=1, tiled=True)  36.7 us
    all_gather x1, waiting for transfers between devices, shards(): whole = lax.all_gather(own_rows, 'mp', axis=1, tiled=True)  31.7 us
    dot_general x1, matrix products, shards(): jnp.einsum('qhd,kd->hqk', query, piece[:, :HD], preferred_element_type=jn...  17.5 us
    dot_general x1, matrix products, shards(): jnp.einsum('hqk,kd->hqd', weights.astype(jnp.bfloat16), piece[:, HD:2 * H...  17.1 us
    reduce_sum x1, other arithmetic, shards(): total = jnp.sum(weights, axis=-1)  15.6 us
  transfers between devices with their start and end apart: 6, of which 4 were waited for; matrix products, arithmetic and copies ran while one was open for 10% of the time, Pallas kernels for 0%

commit v1 on v0

--- a/solution.py
+++ b/solution.py
@@ -11,6 +11,28 @@
 epsilon = 1e-05
 rope_base = 100000000000.0
 negative = -1e30
+
+
+def joined_along(tiles, dim):
+    tiles = jnp.moveaxis(tiles, 0, dim)
+    dims = tiles.shape
+    return tiles.reshape(*dims[:dim], dims[dim] * dims[dim + 1], *dims[dim + 2 :])
+
+
+def ring_gather(array, axis, dim):
+    devices = lax.axis_size(axis)
+    pairs = [(i, (i + 1) % devices) for i in range(devices)]
+    back = [(b, a) for a, b in pairs]
+    lower, upper = ([], [])
+    for step in range(devices - 1):
+        if step % 2 == 0:
+            lower.append(lax.ppermute(lower[-1] if lower else array, axis, pairs))
+        else:
+            upper.append(lax.ppermute(upper[-1] if upper else array, axis, back))
+    blocks = jnp.stack([*lower[::-1], array, *upper])
+    shift = lax.axis_index(axis) - len(lower)
+    blocks = blocks[(jnp.arange(devices) - shift) % devices]
+    return joined_along(blocks, dim)
 
 
 def shifted(block, axis, distance):
@@ -110,7 +132,7 @@
     kv_all, bc_all, cache_all = (
         lax.all_gather(kv_block, "mp", axis=1, tiled=True),
         lax.all_gather(bc_block, "mp", axis=1, tiled=True),
-        lax.all_gather(cache[0], "mp", axis=1, tiled=True),
+        ring_gather(cache[0], "mp", 1),
     )
     inner = jnp.einsum("td,dkc->tkc", normed, w_inner, preferred_element_type=jnp.float32).astype(
         jnp.bfloat16

time: 452 us -> 452 us (level)
  blocking collectives: 65.9 us -> 57.2 us
    all_gather x1 -> x0, blocking collectives: 9.37 us -> none  [shards(): lax.all_gather(cache[0], 'mp', axis=1, tiled=True)]
    ppermute x0 -> x3, waiting for transfers between devices: none -> 5.01 us  [the longest x2 5 us: ring_gather(): lower.append(lax.ppermute(lower[-1] if lower else array, axis, pairs))]
    all_gather x1, waiting for transfers between devices: 39.1 us -> 34.6 us  [prefix(): gathered = jax.tree.map(lambda a: lax.all_gather(a, axis), part)]
  transfers between devices with their start and end apart: 6 -> 9, of which waited for: 4 -> 6; matrix products, arithmetic and copies ran while one was open for 10% -> 11% of each run, Pallas kernels for 0% -> 0%
where the time goes in v1:
time: 452 us; the launch traced here: 449 us
  waiting for transfers between devices  252 us (56%)
  blocking collectives  57.2 us (13%)
  other arithmetic  54 us (12%)
  matrix products  53.6 us (12%)
  between operations  14.9 us (3%)
  starting transfers between devices  9.26 us (2%)
  local copies, waits for them, and re-layouts  7.74 us (2%)
    all_gather x1, waiting for transfers between devices, shards(): piece = lax.all_gather(local_rows, 'seq', axis=0, tiled=True)  143 us
    all_gather x1, blocking collectives, prefix(): gathered = jax.tree.map(lambda a: lax.all_gather(a, axis), part)  38.1 us
    reduce_scatter x1, waiting for transfers between devices, shards(): summed = lax.psum_scatter(term, 'mp', scatter_dimension=1, tiled=True)  36.7 us
    all_gather x1, waiting for transfers between devices, prefix(): gathered = jax.tree.map(lambda a: lax.all_gather(a, axis), part)  34.6 us
    all_gather x1, waiting for transfers between devices, shards(): whole = lax.all_gather(own_rows, 'mp', axis=1, tiled=True)  31.7 us
    dot_general x1, matrix products, shards(): jnp.einsum('qhd,kd->hqk', query, piece[:, :HD], preferred_element_type=jn...  17.3 us
    dot_general x1, matrix products, shards(): jnp.einsum('hqk,kd->hqd', weights.astype(jnp.bfloat16), piece[:, HD:2 * H...  17.1 us
    reduce_sum x1, other arithmetic, shards(): total = jnp.sum(weights, axis=-1)  15.6 us
  transfers between devices with their start and end apart: 9, of which 6 were waited for; matrix products, arithmetic and copies ran while one was open for 11% of the time, Pallas kernels for 0%

profile of v1, /device:TPU:1, one launch (start us, length us, event | category | flops | bytes accessed | tf_op | source)
XLA Modules:
  0.0 449.0 jit_solution(14697746274241853691)
XLA Ops:
  11.0 31.7 %all-gather.9.cloned.1.call-done = bf16[1,256,3072]{2,1,0:T(8,128)(2,1)} async-done(((bf16[1,256,768]{2,1,0:T(8,128)(2,1)}), bf16[1,256,3072]{2,1,0:T(8,128)(2,1)}) %all-gather.9.cloned.1.call-update) | async-done | bytes 1572880 | tf_op jit(solution)/shard_map/all_gather | solution.py:116
  42.7 1.9 fusion.9
  44.7 1.9 fusion.11
  46.6 1.4 fusion.13
  51.5 3.1 collective-permute-start.3
  54.7 2.0 convolution_convert_fusion
  56.6 9.4 %all_gather.25 = bf16[256,512]{1,0:T(8,128)(2,1)S(1)} all-gather(bf16[256,128]{1,0:T(8,128)(2,1)S(1)} %convolution_convert_fusion), channel_id=1, replica_groups=mesh['seq'=32,'mp'=4,'req'=2] {'mp'}, dimensions={1}, use_global_device_ids=true | all-gather | bytes 327680 | tf_op jit(solution)/shard_map/all_gather | solution.py:134
  66.0 3.2 collective-permute-start.4
  71.7 1.3 fusion.46
  73.5 2.4 collective-permute-start.2
  78.1 4.1 collective-permute-done.1
  83.1 1.3 gather_fusion
  85.5 2.3 fusion.102
  89.4 9.8 %all_gather.23 = bf16[256,512]{0,1:T(8,128)(2,1)S(1)} all-gather(bf16[256,128]{0,1:T(8,128)(2,1)S(1)} %fusion.63), channel_id=1, replica_groups=mesh['seq'=32,'mp'=4,'req'=2] {'mp'}, dimensions={1}, use_global_device_ids=true | all-gather | bytes 327680 | tf_op jit(solution)/shard_map/all_gather | solution.py:133
  101.5 1.9 multiply_cosine_fusion
  103.5 15.5 %and_or_fusion = pred[256,16384]{0,1:T(8,128)(4,1)} fusion(s32[256]{0:T(256)S(1)} %iota_add_fusion, s32[16384]{0:T(1024)S(1)} %fusion.82, pred[16384]{0:T(1024)(128)(4,1)S(1)} %get-tuple-element.110, pred[16384]{0:T(1024)(128)(4,1)S(1)} %get-tuple-element.109), kind=kLoop, calls=%fused_computation.10 | loop fusion | flops 12582912 | bytes 4293632 | tf_op jit(solution)/shard_map/or | solution.py:195
  119.9 2.6 fusion.103
  122.8 38.1 %all-gather.2 = f32[32,1,3]{2,1,0:T(1,128)} all-gather(f32[1,1,3]{2,1,0:T(1,128)S(1)} %bitcast.194), channel_id=1, replica_groups=mesh['seq'=32,'mp'=4,'req'=2] {'seq'}, dimensions={0}, use_global_device_ids=true | all-gather | bytes 396 | tf_op jit(solution)/shard_map/all_gather | solution.py:46
  160.9 1.8 subtract_convert_fusion
  163.1 34.6 %all-gather.11.cloned.1.call-done = f32[96,128,256]{2,1,0:T(8,128)} async-done(((f32[3,128,256]{2,1,0:T(8,128)}), f32[96,128,256]{2,1,0:T(8,128)}) %all-gather.11.cloned.1.call-update) | async-done | bytes 12582928 | tf_op jit(solution)/shard_map/all_gather | solution.py:46
  197.9 1.5 convolution_multiply_fusion
  199.5 2.5 multiply_reduce_fusion
  202.2 143.2 %all-gather.7.cloned.1.call-done = bf16[16384,512]{0,1:T(8,128)(2,1)} async-done(((bf16[512,512]{0,1:T(8,128)(2,1)}), bf16[16384,512]{0,1:T(8,128)(2,1)}) %all-gather.7.cloned.1.call-update) | async-done | bytes 16777232 | tf_op jit(solution)/shard_map/all_gather | solution.py:185
  345.4 17.3 %fusion = (f32[2,256]{1,0:T(2,128)S(1)}, f32[16384,256,2]{1,0,2:T(8,128)}) fusion(pred[256,16384]{0,1:T(8,128)(4,1)} %and_or_fusion, bf16[256,2,64]{2,0,1:T(8,128)(2,1)S(1)} %copy-done.9, bf16[256,2,64]{2,0,1:T(8,128)(2,1)S(1)} %copy-done.8, bf16[16384,512]{0,1:T(8,128)(2,1)} %all-gather.7.cloned.1.call-done, s32[]{:T(128)S(6)} %select_n.132), kind=kOutput, calls=%fused_computation.5 | convolution fusion | flops 2172911104 | bytes 42076164 | tf_op jit(solution)/shard_map/qhd,kd->hqk/dot_general | solution.py:197
  362.7 15.6 %fusion.1 = f32[2,256]{1,0:T(2,128)S(1)} fusion(f32[16384,256,2]{1,0,2:T(8,128)} %get-tuple-element.104, f32[2,256]{1,0:T(2,128)S(1)} %broadcast_maximum_fusion, pred[256,16384]{0,1:T(8,128)(4,1)} %and_or_fusion), kind=kLoop, calls=%fused_computation.6 | loop fusion | flops 41942528 | bytes 37752832 | tf_op jit(solution)/shard_map/reduce_sum | solution.py:202
  378.3 17.1 %fusion.27 = bf16[256,2,128]{0,2,1:T(8,128)(2,1)S(1)} fusion(f32[16384,256,2]{1,0,2:T(8,128)} %get-tuple-element.104, f32[2,256]{1,0:T(2,128)S(1)} %broadcast_maximum_fusion, pred[256,16384]{0,1:T(8,128)(4,1)} %and_or_fusion, bf16[16384,512]{0,1:T(8,128)(2,1)} %all-gather.7.cloned.1.call-done, s32[]{:T(128)S(6)} %add.255, f32[256,2]{0,1:T(2,128)S(1)} %bitcast.193), kind=kOutput, calls=%fused_computation.33 | convolution fusion | flops 2189557760 | bytes 42078212 | tf_op jit(solution)/shard_map/hqk,kd->hqd/dot_general | solution.py:203
  395.4 2.0 fusion.104
  397.5 2.7 convolution_add_fusion
  400.2 1.6 copy.64
  401.9 1.9 add_bitcast_fusion
  403.7 36.7 %reduce-scatter.2.cloned.1.call-done = f32[256,768]{1,0:T(8,128)} async-done(((f32[256,3072]{1,0:T(8,128)}), f32[256,768]{1,0:T(8,128)}) %reduce-scatter.2.cloned.1.call-update) | async-done | bytes 786448 | tf_op jit(solution)/shard_map/reduce_scatter | solution.py:214
  440.5 1.9 fusion.40
  (114 shorter events, 19.7 us)
Async XLA Ops:
  7.2 390.3 %copy-start = (bf16[384,3072]{1,0:T(8,128)(2,1)S(1)}, bf16[384,3072]{1,0:T(8,128)(2,1)}, u32[]{:S(2)}) copy-start(bf16[384,3072]{1,0:T(8,128)(2,1)} %param.36) | copy-start | bytes 7077892
  7.2 35.5 %all-gather.9.cloned.1.call-start = ((), (), s32[]{:S(2)}) async-start(), calls=%async_computation.3 | async-start | bytes 1966080 | tf_op jit(solution)/shard_map/all_gather | solution.py:116
  7.9 189.8 %all-gather.11.cloned.1.call-start = ((), (), s32[]{:S(2)}) async-start(), calls=%async_computation.4 | async-start | bytes 12976128 | tf_op jit(solution)/shard_map/all_gather | solution.py:46
  42.7 3.9 copy-start.22
  46.6 2.4 copy-start.1
  46.6 2.4 copy-start.13
  46.6 2.4 copy-start.21
  46.6 8.0 %copy-start.6 = (bf16[3072,128]{1,0:T(8,128)(2,1)S(1)}, bf16[3072,128]{1,0:T(8,128)(2,1)}, u32[]{:S(2)}) copy-start(bf16[3072,128]{1,0:T(8,128)(2,1)} %param.28) | copy-start | bytes 2359300
  48.1 21.8 %copy-start.16 = (bf16[1,3,384]{2,1,0:T(4,128)(2,1)S(1)}, bf16[1,3,384]{2,1,0:T(4,128)(2,1)}, u32[]{:S(2)}) copy-start(bf16[1,3,384]{2,1,0:T(4,128)(2,1)} %param.39) | copy-start | bytes 6916
  48.1 23.2 %copy-start.15 = (bf16[1,3,512]{2,1,0:T(4,128)(2,1)S(1)}, bf16[1,3,512]{2,1,0:T(4,128)(2,1)}, u32[]{:S(2)}) copy-start(bf16[1,3,512]{2,1,0:T(4,128)(2,1)} %param.40) | copy-start | bytes 9220
  51.5 20.2 %copy-start.18 = (f32[3]{0:T(128)}, f32[3]{0:T(128)S(1)}, u32[]{:S(2)}) copy-start(f32[3]{0:T(128)S(1)} %get-tuple-element.66) | copy-start | bytes 40
  51.5 18.3 %collective-permute-start.3 = (bf16[3,384]{1,0:T(4,128)(2,1)S(1)}, bf16[3,384]{1,0:T(4,128)(2,1)S(1)}, u32[]{:S(2)}, u32[]{:S(2)}) collective-permute-start(bf16[3,384]{1,0:T(4,128)(2,1)S(1)} %slice_bitcast_fusion.1), channel_id=1, source_target_pairs={{0,8},{8,16},{16,24},{24,32},{32,40},{40,48},{48,56},{56,64},{64,7... | collective-permute-start | bytes 6920 | tf_op jit(solution)/shard_map/ppermute | solution.py:41
  66.0 7.1 %copy-start.10 = (bf16[1,256,128]{2,1,0:T(8,128)(2,1)S(1)}, bf16[1,256,128]{2,1,0:T(8,128)(2,1)}, u32[]{:S(2)}) copy-start(bf16[1,256,128]{2,1,0:T(8,128)(2,1)} %param.37) | copy-start | bytes 196612
  66.0 5.3 %collective-permute-start.4 = (bf16[3,512]{1,0:T(4,128)(2,1)S(1)}, bf16[3,512]{1,0:T(4,128)(2,1)S(1)}, u32[]{:S(2)}, u32[]{:S(2)}) collective-permute-start(bf16[3,512]{1,0:T(4,128)(2,1)S(1)} %slice.138), channel_id=1, source_target_pairs={{0,8},{8,16},{16,24},{24,32},{32,40},{40,48},{48,56},{56,64},{64,7... | collective-permute-start | bytes 9224 | tf_op jit(solution)/shard_map/ppermute | solution.py:41
  71.3 16.5 %copy-start.4 = (f32[256,384]{0,1:T(8,128)}, f32[256,384]{0,1:T(8,128)S(1)}, u32[]{:S(2)}) copy-start(f32[256,384]{0,1:T(8,128)S(1)} %copy.58) | copy-start | bytes 1179652
  73.0 272.4 %all-gather.7.cloned.1.call-start = ((), (), s32[]{:S(2)}) async-start(), calls=%async_computation.1 | async-start | bytes 17301504 | tf_op jit(solution)/shard_map/all_gather | solution.py:185
  73.1 4.4 collective-permute-start
  73.5 4.6 %collective-permute-start.2 = (bf16[256,128]{1,0:T(8,128)(2,1)S(1)}, bf16[256,128]{1,0:T(8,128)(2,1)S(1)}, u32[]{:S(2)}, u32[]{:S(2)}) collective-permute-start(bf16[256,128]{1,0:T(8,128)(2,1)S(1)} %bitcast.181), channel_id=1, source_target_pairs={{2,0},{4,2},{6,4},{0,6},{3,1},{5,3},{7,5},{1,7},{10,8},{12,10},{14... | collective-permute-start | bytes 196616 | tf_op jit(solution)/shard_map/ppermute | solution.py:31
  76.5 23.6 %copy-start.14 = (f32[256]{0:T(256)}, f32[256]{0:T(256)S(1)}, u32[]{:S(2)}) copy-start(f32[256]{0:T(256)S(1)} %add_convert_fusion.1) | copy-start | bytes 3076
  77.5 4.6 %copy-start.11 = (bf16[256,128]{1,0:T(8,128)(2,1)}, bf16[256,128]{1,0:T(8,128)(2,1)S(1)}, u32[]{:S(2)}) copy-start(bf16[256,128]{1,0:T(8,128)(2,1)S(1)} %collective-permute-done) | copy-start | bytes 196612
  77.5 4.6 %collective-permute-start.1 = (bf16[256,128]{1,0:T(8,128)(2,1)S(1)}, bf16[256,128]{1,0:T(8,128)(2,1)S(1)}, u32[]{:S(2)}, u32[]{:S(2)}) collective-permute-start(bf16[256,128]{1,0:T(8,128)(2,1)S(1)} %collective-permute-done), channel_id=1, source_target_pairs={{0,2},{2,4},{4,6},{6,0},{1,3},{3,5},{5,7},{7,1},{8,10},{10,12},{12... | collective-permute-start | bytes 196616 | tf_op jit(solution)/shard_map/ppermute | solution.py:29
  78.1 4.1 copy-start.12
  84.4 17.2 %copy-start.17 = (f32[64]{0:T(128)S(1)}, f32[64]{0:T(128)}, u32[]{:S(2)}) copy-start(f32[64]{0:T(128)} %multiply_power_fusion) | copy-start | bytes 772
  87.8 31.2 %copy-start.5 = (f32[256,1,384]{2,0,1:T(8,128)S(1)}, f32[256,1,384]{2,0,1:T(8,128)}, u32[]{:S(2)}) copy-start(f32[256,1,384]{2,0,1:T(8,128)} %get-tuple-element.88) | copy-start | bytes 1179652
  88.8 0.6 copy-start.7
  100.1 340.4 %reduce-scatter.2.cloned.1.call-start = ((), (), s32[]{:S(2)}) async-start(), calls=%async_computation.2 | async-start | bytes 3932160 | tf_op jit(solution)/shard_map/reduce_scatter | solution.py:214
  103.5 19.3 %copy-start.20 = (f32[3]{0:T(128)S(1)}, f32[3]{0:T(128)}, u32[]{:S(2)}) copy-start(f32[3]{0:T(128)} %get-tuple-element.67) | copy-start | bytes 40
  199.5 146.0 %copy-start.8 = (bf16[256,2,64]{2,0,1:T(8,128)(2,1)S(1)}, bf16[256,2,64]{2,0,1:T(8,128)(2,1)}, u32[]{:S(2)}) copy-start(bf16[256,2,64]{2,0,1:T(8,128)(2,1)} %get-tuple-element.86) | copy-start | bytes 196612
  199.5 146.0 %copy-start.9 = (bf16[256,2,64]{2,0,1:T(8,128)(2,1)S(1)}, bf16[256,2,64]{2,0,1:T(8,128)(2,1)}, u32[]{:S(2)}) copy-start(bf16[256,2,64]{2,0,1:T(8,128)(2,1)} %get-tuple-element.87) | copy-start | bytes 196612
  397.5 2.8 copy-start.19
  397.5 4.4 copy-start.2
  400.2 40.3 %copy-start.3 = (bf16[1,256,768]{2,1,0:T(8,128)(2,1)S(1)}, bf16[1,256,768]{2,1,0:T(8,128)(2,1)}, u32[]{:S(2)}) copy-start(bf16[1,256,768]{2,1,0:T(8,128)(2,1)} %param.22) | copy-start | bytes 1179652
Sparse Core Ops, SparseCore 0:
  9.8 32.8 all-gather.8
  73.1 124.4 all-gather.10
  200.2 145.2 all-gather.6
  400.3 40.0 reduce-scatter.1
